TPU v7x, 32 devices: a whole 2x2x4 slice. The times are simulated.
32 devices in a mesh: rep: 1, fsdp: 32 (over z, y, x, core).
Axes of the slice: x: 2, y: 2, z: 4, core: 2. Of those that a mesh axis runs over, the one named last changes fastest.
Arguments:
- tokens: bfloat16 [24576, 4096], P(('rep', 'fsdp')), may hold values from -6 to 6
- cotangent: bfloat16 [24576, 512], P(('rep', 'fsdp')), may hold values from -0.0390625 to 0.0390625
- policy: float32 [4096, 512], P('fsdp'), may hold values from -0.09375 to 0.09375
- anchor: float32 [4096, 512], P('fsdp'), may hold values from -0.09375 to 0.09375
- moment: float32 [4096, 512], P('fsdp'), may hold values from -3 to 3
- second: float32 [4096, 512], P('fsdp'), may hold values from 0.25 to 4
- readout: float32 [512], replicated, may hold values from -6 to 6
- pair_index: int32 [64, 2], P(('rep', 'fsdp')), may hold values from 0 to 127, as said below
- noisy_flags: int32 [64], P(('rep', 'fsdp')), may hold values 0 or 1
Outputs:
- policy_next: float32 [4096, 512], P('fsdp')
- anchor_next: float32 [4096, 512], P('fsdp')
- moment_next: float32 [4096, 512], P('fsdp')
- second_next: float32 [4096, 512], P('fsdp')
- pair_loss: float32 [64], P(('rep', 'fsdp'))
Inputs may be any that keep to these rules, and one draw needn't show every extreme that they name: Each of the 128 sequences appears exactly once in pair_index.
All inputs are finite; a program needn't handle non-finite values. No bound on the sum of `noisy_flags` on one device may be relied on, other than what follows from the above.
Results may differ from a plain program's by a relative error of at most 0.0025.
Values may be sent and summed in bfloat16 or wider, within the bound.
A program may use at most 64 MiB of HBM per device.

v0:
```python
import jax
import jax.numpy as jnp
from jax import lax
from jax.sharding import PartitionSpec as P

LEN = 192


beta_one = 0.9
beta_two = 0.95
step_count = 20
learn_rate = 0.003
adam_epsilon = 1e-08
blend_rate = 0.6
smoothing = 0.1


def adam_update(gradient, policy, anchor, moment, second):
    moment_new = beta_one * moment + (1.0 - beta_one) * gradient
    second_new = beta_two * second + (1.0 - beta_two) * gradient * gradient
    correct_one = 1.0 - beta_one**step_count
    correct_two = 1.0 - beta_two**step_count
    policy_new = policy - learn_rate * (moment_new / correct_one) / (
        jnp.sqrt(second_new / correct_two) + adam_epsilon
    )
    anchor_new = blend_rate * policy_new + (1.0 - blend_rate) * anchor
    return (policy_new, anchor_new, moment_new, second_new)


def token_scores(values, readout):
    return jnp.sum(jax.nn.log_sigmoid(values * readout[None, :]), axis=1)


def sequence_margin(policy_values, anchor_values, readout, sequence_length):
    token_gap = token_scores(policy_values, readout) - token_scores(anchor_values, readout)
    return jnp.mean(token_gap.reshape(-1, sequence_length), axis=1)


def pair_losses(margins, pair_index, noisy_flags):
    sequence_index = jnp.arange(margins.shape[0], dtype=jnp.int32)
    chosen = jnp.sum(
        jnp.where(pair_index[:, 0:1] == sequence_index[None, :], margins[None, :], 0.0), axis=1
    )
    rejected = jnp.sum(
        jnp.where(pair_index[:, 1:2] == sequence_index[None, :], margins[None, :], 0.0), axis=1
    )
    margin_gap = chosen - rejected
    logit_value = jnp.where(noisy_flags == 1, -margin_gap, margin_gap)
    return -(1.0 - smoothing) * jax.nn.log_sigmoid(logit_value) - smoothing * jax.nn.log_sigmoid(
        -logit_value
    )


def shards(tokens, cotangent, policy, anchor, moment, second, readout, pair_index, noisy_flags):
    part_sum = lax.psum_scatter(
        lax.dot_general(
            tokens, cotangent, (((0,), (0,)), ((), ())), preferred_element_type=jnp.float32
        ),
        "fsdp",
        scatter_dimension=0,
        tiled=True,
    )
    gradient = lax.psum(part_sum.astype(jnp.bfloat16), "rep").astype(jnp.float32)
    policy_next, anchor_next, moment_next, second_next = adam_update(
        gradient, policy, anchor, moment, second
    )
    policy_half = policy_next.astype(jnp.bfloat16)
    anchor_half = anchor_next.astype(jnp.bfloat16)
    policy_whole = lax.all_gather(policy_half, "fsdp", axis=0, tiled=True)
    anchor_whole = lax.all_gather(anchor_half, "fsdp", axis=0, tiled=True)
    policy_values = jnp.dot(tokens, policy_whole, preferred_element_type=jnp.float32)
    anchor_values = jnp.dot(tokens, anchor_whole, preferred_element_type=jnp.float32)
    margins_own = sequence_margin(policy_values, anchor_values, readout, LEN)
    all_margins = lax.all_gather(margins_own, ("rep", "fsdp"), axis=0, tiled=True)
    pair_loss = pair_losses(all_margins, pair_index, noisy_flags)
    return (policy_next, anchor_next, moment_next, second_next, pair_loss)


def solution(mesh):
    placed = (
        P(("rep", "fsdp"), None),
        P(("rep", "fsdp"), None),
        P("fsdp", None),
        P("fsdp", None),
        P("fsdp", None),
        P("fsdp", None),
        P(),
        P(("rep", "fsdp"), None),
        P(("rep", "fsdp")),
    )
    return jax.shard_map(
        shards,
        mesh=mesh,
        in_specs=placed,
        out_specs=(
            P("fsdp", None),
            P("fsdp", None),
            P("fsdp", None),
            P("fsdp", None),
            P(("rep", "fsdp")),
        ),
        check_vma=False,
    )
```

profile of v0, /device:TPU:0, one launch (start us, length us, event | category | flops | bytes accessed | tf_op | source)
XLA Modules:
  0.0 349.1 jit_solution(543226344845690600)
XLA Ops:
  7.2 0.0 copy-start
  7.2 0.0 reduce-scatter.2.cloned.1.call-start
  7.2 1.1 copy-done
  8.3 8.6 %fusion.20 = f32[4096,512]{1,0:T(8,128)} fusion(bf16[768,4096]{1,0:T(8,128)(2,1)} %param.9, bf16[768,512]{1,0:T(8,128)(2,1)S(1)} %copy-done), kind=kOutput, calls=%fused_computation.38 | convolution fusion | flops 3221225472 | bytes 15466496 | tf_op jit(solution)/shard_map/dot_general | solution.py:56
  16.9 0.0 copy-start.2
  16.9 0.0 copy-start.3
  16.9 0.0 copy-start.4
  16.9 0.0 reduce-scatter.2.cloned.1.call-update
  16.9 0.0 copy-start.5
  16.9 0.0 copy-start.6
  16.9 0.0 copy-start.8
  16.9 0.0 all-gather.5.cloned.1.call-start
  17.0 153.2 %reduce-scatter.2.cloned.1.call-done = f32[128,512]{1,0:T(8,128)} async-done(((f32[4096,512]{1,0:T(8,128)}), f32[128,512]{1,0:T(8,128)}) %reduce-scatter.2.cloned.1.call-update) | async-done | bytes 262160 | tf_op jit(solution)/shard_map/reduce_scatter | solution.py:55
  170.2 0.0 copy-done.2
  170.2 0.0 copy-done.3
  170.2 0.0 copy-done.4
  170.2 1.9 fusion.16
  172.1 0.0 copy-start.1
  172.1 0.0 copy-done.5
  172.1 0.8 fusion.19
  172.9 0.0 all-gather.5.cloned.1.call-update
  173.0 0.0 all-gather.3.cloned.1.call-start
  173.0 0.7 all-gather.3.cloned.1.call-update
  173.7 0.0 copy-done.6
  173.7 0.2 slice_reduce_fusion
  173.9 56.8 %all-gather.5.cloned.1.call-done = bf16[4096,512]{1,0:T(8,128)(2,1)} async-done(((bf16[128,512]{1,0:T(8,128)(2,1)}), bf16[4096,512]{1,0:T(8,128)(2,1)}) %all-gather.5.cloned.1.call-update) | async-done | bytes 4194320 | tf_op jit(solution)/shard_map/all_gather | solution.py:70
  230.7 0.0 copy-done.8
  230.7 8.4 %fusion.1 = f32[768]{0:T(1024)S(1)} fusion(bf16[4096,512]{1,0:T(8,128)(2,1)} %all-gather.5.cloned.1.call-done, bf16[768,4096]{1,0:T(8,128)(2,1)} %param.9, f32[512]{0:T(512)S(1)} %copy-done.8), kind=kOutput, calls=%fused_computation.3 | convolution fusion | flops 3224763648 | bytes 10490880 | tf_op jit(solution)/shard_map/dot_general | solution.py:72
  239.1 0.0 copy-done.1
  239.1 0.0 copy-start.7
  239.1 54.9 %all-gather.3.cloned.1.call-done = bf16[4096,512]{1,0:T(8,128)(2,1)} async-done(((bf16[128,512]{1,0:T(8,128)(2,1)}), bf16[4096,512]{1,0:T(8,128)(2,1)}) %all-gather.3.cloned.1.call-update) | async-done | bytes 4194320 | tf_op jit(solution)/shard_map/all_gather | solution.py:69
  294.0 8.4 %fusion = f32[768]{0:T(1024)S(1)} fusion(bf16[4096,512]{1,0:T(8,128)(2,1)} %all-gather.3.cloned.1.call-done, bf16[768,4096]{1,0:T(8,128)(2,1)} %param.9, f32[512]{0:T(512)S(1)} %copy-done.8), kind=kOutput, calls=%fused_computation.2 | convolution fusion | flops 3224763648 | bytes 10490880 | tf_op jit(solution)/shard_map/dot_general | solution.py:71
  302.4 0.1 sub.18
  302.5 0.1 reduce_sum.47
  302.6 0.1 multiply_dynamic-update-slice_fusion
  302.7 39.1 %all-reduce = f32[128]{0:T(128)S(1)} all-reduce(f32[128]{0:T(128)S(1)} %multiply_dynamic-update-slice_fusion), channel_id=1, replica_groups=mesh['rep'=1,'fsdp'=32] {'rep','fsdp'}, use_global_device_ids=true, to_apply=%add | all-reduce | flops 128 | bytes 1024
  341.8 0.2 fusion.13
  342.0 0.0 copy-done.7
  342.0 0.5 multiply_subtract_fusion
  (2 shorter events, 0.0 us)
Async XLA Ops:
  7.2 1.1 copy-start
  7.2 163.0 %reduce-scatter.2.cloned.1.call-start = ((), (), s32[]{:S(2)}) async-start(), calls=%async_computation.1 | async-start | bytes 8650752 | tf_op jit(solution)/shard_map/reduce_scatter | solution.py:55
  16.9 153.3 %copy-start.2 = (f32[128,512]{1,0:T(8,128)S(1)}, f32[128,512]{1,0:T(8,128)}, u32[]{:S(2)}) copy-start(f32[128,512]{1,0:T(8,128)} %param.11) | copy-start | bytes 786436
  16.9 153.3 %copy-start.3 = (f32[128,512]{1,0:T(8,128)S(1)}, f32[128,512]{1,0:T(8,128)}, u32[]{:S(2)}) copy-start(f32[128,512]{1,0:T(8,128)} %param.13) | copy-start | bytes 786436
  16.9 153.3 %copy-start.4 = (f32[128,512]{1,0:T(8,128)S(1)}, f32[128,512]{1,0:T(8,128)}, u32[]{:S(2)}) copy-start(f32[128,512]{1,0:T(8,128)} %param.14) | copy-start | bytes 786436
  16.9 155.2 %copy-start.5 = (f32[128,512]{1,0:T(8,128)S(1)}, f32[128,512]{1,0:T(8,128)}, u32[]{:S(2)}) copy-start(f32[128,512]{1,0:T(8,128)} %param.12) | copy-start | bytes 786436
  16.9 156.8 %copy-start.6 = (s32[2,2]{1,0:T(2,128)S(1)}, s32[2,2]{1,0:T(2,128)}, u32[]{:S(2)}) copy-start(s32[2,2]{1,0:T(2,128)} %param.16) | copy-start | bytes 52
  16.9 213.8 %copy-start.8 = (f32[512]{0:T(512)S(1)}, f32[512]{0:T(512)}, u32[]{:S(2)}) copy-start(f32[512]{0:T(512)} %param.15) | copy-start | bytes 6148
  16.9 213.8 %all-gather.5.cloned.1.call-start = ((), (), s32[]{:S(2)}) async-start(), calls=%async_computation.3 | async-start | bytes 4325376 | tf_op jit(solution)/shard_map/all_gather | solution.py:70
  172.1 67.0 %copy-start.1 = (f32[128,512]{1,0:T(8,128)}, f32[128,512]{1,0:T(8,128)S(1)}, u32[]{:S(2)}) copy-start(f32[128,512]{1,0:T(8,128)S(1)} %get-tuple-element.10) | copy-start | bytes 786436
  173.0 121.0 %all-gather.3.cloned.1.call-start = ((), (), s32[]{:S(2)}) async-start(), calls=%async_computation.2 | async-start | bytes 4325376 | tf_op jit(solution)/shard_map/all_gather | solution.py:69
  239.1 102.9 %copy-start.7 = (s32[2]{0:T(128)S(1)}, s32[2]{0:T(128)}, u32[]{:S(2)}) copy-start(s32[2]{0:T(128)} %param.17) | copy-start | bytes 28
Sparse Core Ops, SparseCore 0:
  17.0 153.1 reduce-scatter.1
  173.1 57.5 all-gather.4
  233.6 60.3 all-gather.2
where the time goes:
time: 349 us
  waiting for transfers between devices  266 us (76%)
  blocking collectives  39.1 us (11%)
  matrix products  25.3 us (7%)
  between operations  13.8 us (4%)
  other arithmetic  3.69 us (1%)
    reduce_scatter x1, waiting for transfers between devices, shards(): lax.psum_scatter(lax.dot_general(tokens, cotangent, (((0,), (0,)), ((), (...  153 us
    all_gather x1, waiting for transfers between devices, shards(): anchor_whole = lax.all_gather(anchor_half, 'fsdp', axis=0, tiled=True)  56.8 us
    all_gather x1, waiting for transfers between devices, shards(): policy_whole = lax.all_gather(policy_half, 'fsdp', axis=0, tiled=True)  54.9 us
    unnamed x1, blocking collectives  39.1 us
    dot_general x1, matrix products, shards(): lax.dot_general(tokens, cotangent, (((0,), (0,)), ((), ())), preferred_el...  8.57 us
    dot_general x1, matrix products, shards(): jnp.dot(tokens, anchor_whole, preferred_element_type=jnp.float32)  8.39 us
    dot_general x1, matrix products, shards(): jnp.dot(tokens, policy_whole, preferred_element_type=jnp.float32)  8.38 us
  transfers between devices with their start and end apart: 3, of which 3 were waited for; matrix products, arithmetic and copies ran while one was open for 2% of the time, Pallas kernels for 0%

commit v1 on v0

--- a/solution.py
+++ b/solution.py
@@ -1,6 +1,9 @@
+import functools
 import jax
 import jax.numpy as jnp
 from jax import lax
+from jax.experimental import pallas as pl
+from jax.experimental.pallas import tpu as pltpu
 from jax.sharding import PartitionSpec as P
 
 LEN = 192
@@ -73,6 +76,462 @@
     margins_own = sequence_margin(policy_values, anchor_values, readout, LEN)
     all_margins = lax.all_gather(margins_own, ("rep", "fsdp"), axis=0, tiled=True)
     pair_loss = pair_losses(all_margins, pair_index, noisy_flags)
+    return (policy_next, anchor_next, moment_next, second_next, pair_loss)
+
+
+STEP_ORDER = (2, 1, 3, 0)
+MESH_ID = pl.DeviceIdType.MESH
+
+
+def fused_kernel(
+    sizes,
+    tokens,
+    cotangent,
+    policy,
+    anchor,
+    moment,
+    second,
+    readout,
+    policy_out,
+    anchor_out,
+    moment_out,
+    second_out,
+    margin_out,
+    tok,
+    cot,
+    cot_t,
+    par,
+    send_a1,
+    recv_a1,
+    keep_a,
+    send_b1,
+    recv_b1,
+    keep_b,
+    send_a2,
+    recv_a2,
+    send_b2,
+    recv_b2,
+    send_z,
+    recv_z,
+    grad_own,
+    result,
+    weights,
+    acc,
+    score_own,
+    score_pair,
+    table,
+    local_sem,
+    swap_send,
+    swap_recv,
+    rs_send,
+    rs_recv,
+    out_send,
+    out_recv,
+    z_send,
+    z_recv,
+    g2_send,
+    g2_recv,
+    g3_send,
+    g3_recv,
+    m_send,
+    m_recv,
+):
+    n, rows, tokens_own, half, depth, seq_own = sizes
+    block = 2 * rows
+    span = 4 * block
+    low = half // 2
+    me = lax.axis_index("fsdp")
+    core = me % 2
+    px = (me // 2) % 2
+    py = (me // 4) % 2
+    pz = me // 8
+    chip = me // 2
+    mate = me + 1 - 2 * core
+    x_mate = me + 2 - 4 * px
+    y_mate = me + 4 - 8 * py
+
+    def z_mate(shift):
+        return (me + 8 * shift) % n
+
+    def remote(src, dst, send_sem, recv_sem, device):
+        return pltpu.make_async_remote_copy(
+            src_ref=src,
+            dst_ref=dst,
+            send_sem=send_sem,
+            recv_sem=recv_sem,
+            device_id={"fsdp": device},
+            device_id_type=MESH_ID,
+        )
+
+    barrier = pltpu.get_barrier_semaphore()
+    others = [mate, x_mate, y_mate] + [z_mate(s) for s in (1, 2, 3)]
+    for other in others:
+        pl.semaphore_signal(barrier, inc=1, device_id={"fsdp": other}, device_id_type=MESH_ID)
+
+    mine = pl.ds(pl.multiple_of(core * half, half), half)
+    theirs = pl.ds(pl.multiple_of((1 - core) * half, half), half)
+    params = (policy, anchor, moment, second)
+
+    def columns(s):
+        z_to = (pz + s) % 4
+        return pl.ds(pl.multiple_of(z_to * span, span), span)
+
+    cot_local = pltpu.make_async_copy(cotangent.at[:, mine], cot.at[core], local_sem.at[4])
+    cot_local.start()
+    tok_local = {}
+    for s in STEP_ORDER:
+        tok_local[s] = pltpu.make_async_copy(
+            tokens.at[:, columns(s)], tok.at[core, :, columns(s)], local_sem.at[s]
+        )
+        tok_local[s].start()
+    par_local = []
+    for a in range(4):
+        copy = pltpu.make_async_copy(params[a].at[:, mine], par.at[a, core], local_sem.at[5 + a])
+        copy.start()
+        par_local.append(copy)
+
+    pl.semaphore_wait(barrier, len(others))
+
+    sends = []
+    cot_swap = remote(cotangent.at[:, theirs], cot.at[core], swap_send.at[4], swap_recv.at[4], mate)
+    cot_swap.start()
+    sends.append(cot_swap)
+    tok_swap = {}
+    for s in STEP_ORDER:
+        tok_swap[s] = remote(
+            tokens.at[:, columns(s)],
+            tok.at[core, :, columns(s)],
+            swap_send.at[s],
+            swap_recv.at[s],
+            mate,
+        )
+        tok_swap[s].start()
+        sends.append(tok_swap[s])
+    par_swap = []
+    for a in range(4):
+        copy = remote(
+            params[a].at[:, theirs], par.at[a, core], swap_send.at[5 + a], swap_recv.at[5 + a], mate
+        )
+        copy.start()
+        par_swap.append(copy)
+        sends.append(copy)
+
+    cot_local.wait()
+    cot_swap.wait_recv()
+    for r in range(2):
+        cot_t[:, r * tokens_own : (r + 1) * tokens_own] = (
+            cot[r].astype(jnp.float32).T.astype(jnp.bfloat16)
+        )
+
+    def first(s):
+        tok_local[s].wait()
+        tok_swap[s].wait_recv()
+
+    def block_gradient(s, dy, dx):
+        target = ((pz + s) % 4) * 4 + ((py + dy) % 2) * 2 + (px + dx) % 2
+        where = pl.ds(pl.multiple_of(target * block, block), block)
+        total = jnp.dot(
+            cot_t[:, :tokens_own], tok[0, :, where], preferred_element_type=jnp.float32
+        )
+        total += jnp.dot(
+            cot_t[:, tokens_own:], tok[1, :, where], preferred_element_type=jnp.float32
+        )
+        if dx == 1:
+            send_a1[s, dy] = total[:low].astype(jnp.bfloat16)
+        else:
+            keep_a[s, dy] = total[:low]
+        if dy == 1:
+            send_b1[s, dx] = total[low:].astype(jnp.bfloat16)
+        else:
+            keep_b[s, dx] = total[low:]
+
+    hops = {}
+
+    def hop(name, s, slot, src, dst, device):
+        copy = remote(src, dst, rs_send.at[slot, s], rs_recv.at[slot, s], device)
+        copy.start()
+        hops[name, s] = copy
+        sends.append(copy)
+
+    def stage_one(s):
+        first(s)
+        block_gradient(s, 1, 1)
+        block_gradient(s, 0, 1)
+        hop("a1", s, 0, send_a1.at[s], recv_a1.at[s], x_mate)
+        block_gradient(s, 1, 0)
+        hop("b1", s, 1, send_b1.at[s], recv_b1.at[s], y_mate)
+        block_gradient(s, 0, 0)
+
+    def stage_two(s):
+        hops["a1", s].wait_recv()
+        send_a2[s] = (keep_a[s, 1] + recv_a1[s, 1].astype(jnp.float32)).astype(jnp.bfloat16)
+        hop("a2", s, 2, send_a2.at[s], recv_a2.at[s], y_mate)
+        hops["b1", s].wait_recv()
+        send_b2[s] = (keep_b[s, 1] + recv_b1[s, 1].astype(jnp.float32)).astype(jnp.bfloat16)
+        hop("b2", s, 3, send_b2.at[s], recv_b2.at[s], x_mate)
+
+    def stage_three(s):
+        hops["a2", s].wait_recv()
+        total_a = keep_a[s, 0] + recv_a1[s, 0].astype(jnp.float32) + recv_a2[s].astype(jnp.float32)
+        hops["b2", s].wait_recv()
+        total_b = keep_b[s, 0] + recv_b1[s, 0].astype(jnp.float32) + recv_b2[s].astype(jnp.float32)
+        if s == 0:
+            grad_own[:low] = total_a
+            grad_own[low:] = total_b
+        else:
+            send_z[s - 1, :low] = total_a.astype(jnp.bfloat16)
+            send_z[s - 1, low:] = total_b.astype(jnp.bfloat16)
+            hop("z", s, 4, send_z.at[s - 1], recv_z.at[s - 1], z_mate(s))
+
+    for i in range(len(STEP_ORDER) + 2):
+        if i < len(STEP_ORDER):
+            stage_one(STEP_ORDER[i])
+        if 1 <= i <= len(STEP_ORDER):
+            stage_two(STEP_ORDER[i - 1])
+        if i >= 2:
+            stage_three(STEP_ORDER[i - 2])
+
+    for a in range(4):
+        par_local[a].wait()
+        par_swap[a].wait_recv()
+    for s in STEP_ORDER[:3]:
+        hops["z", s].wait_recv()
+    gradient = grad_own[...]
+    for s in range(3):
+        gradient += recv_z[s].astype(jnp.float32)
+    gradient = gradient.T
+    home = chip * block
+    for r in range(2):
+        updated = adam_update(
+            gradient[r * rows : (r + 1) * rows], par[0, r], par[1, r], par[2, r], par[3, r]
+        )
+        for a in range(4):
+            result[a, r] = updated[a]
+        for m in range(2):
+            weights[m, pl.ds(pl.multiple_of(home + r * rows, rows), rows), :] = updated[m].astype(
+                jnp.bfloat16
+            )
+
+    top = pz // 2
+    near = pz + top * (3 - 2 * pz)
+
+    def source(t):
+        there = (near, 1 - near, 2, 3)[t]
+        return there + top * (3 - 2 * there)
+
+    def part(m, k):
+        return weights.at[m, pl.ds(pl.multiple_of(k * block, block), block), :]
+
+    def z_copy(m, zz, way):
+        ref = part(m, zz * 4 + py * 2 + px)
+        device = z_mate(1) if way == 0 else z_mate(3)
+        return remote(ref, ref, z_send.at[way, m, zz], z_recv.at[m, zz], device)
+
+    def z_forward(zz, act):
+        @pl.when(jnp.logical_and(zz <= pz, pz < 3))
+        def _():
+            for m in range(2):
+                act(z_copy(m, zz, 0))
+
+        @pl.when(jnp.logical_and(zz >= pz, pz > 0))
+        def _():
+            for m in range(2):
+                act(z_copy(m, zz, 1))
+
+    gathers = {}
+
+    def gather_two(t, zz):
+        for m in range(2):
+            ref = part(m, zz * 4 + py * 2 + px)
+            device = y_mate if m == 0 else x_mate
+            copy = remote(ref, ref, g2_send.at[t, m], g2_recv.at[t, m], device)
+            copy.start()
+            gathers[2, t, m] = copy
+            sends.append(copy)
+
+    def gather_three(t, zz, late, m):
+        ky = (py + late) % 2 if m == 0 else py
+        kx = px if m == 0 else (px + late) % 2
+        ref = part(m, zz * 4 + ky * 2 + kx)
+        device = x_mate if m == 0 else y_mate
+        copy = remote(ref, ref, g3_send.at[t, late, m], g3_recv.at[t, late, m], device)
+        copy.start()
+        gathers[3, t, late, m] = copy
+        sends.append(copy)
+
+    tile = tokens_own // 2
+    scale = readout[core]
+
+    def score_sum(values):
+        low_part = jnp.minimum(values, 0.0).reshape(LEN // 8, 8, half)
+        factor = (1.0 + jnp.exp(-jnp.abs(values))).reshape(LEN // 8, 8, half)
+        product = factor[0]
+        for j in range(1, LEN // 8):
+            product = product * factor[j]
+        return jnp.sum(low_part, axis=0) - jnp.log(product)
+
+    def compute(t, zz):
+        for late in range(2):
+            for m in range(2):
+                gathers[3, t, late, m].wait_recv()
+        where = pl.ds(pl.multiple_of(zz * span, span), span)
+
+        @pl.loop(0, 4)
+        def _(i):
+            r = i // 2
+            at = pl.ds(pl.multiple_of((i % 2) * tile, tile), tile)
+            lhs = tok[r, at, where]
+            values = []
+            for m in range(2):
+                value = jnp.dot(lhs, weights[m, where, :], preferred_element_type=jnp.float32)
+                if t > 0:
+                    value = value + acc[m, i]
+                if t < 3:
+                    acc[m, i] = value
+                else:
+                    acc[m, i] = value * scale
+            if t == 3:
+                for j in range(tile // LEN):
+                    gap = score_sum(acc[0, i, j * LEN : (j + 1) * LEN]) - score_sum(
+                        acc[1, i, j * LEN : (j + 1) * LEN]
+                    )
+                    gap = jnp.sum(gap, axis=0, keepdims=True)
+                    gap = jnp.sum(gap, axis=1, keepdims=True)
+                    score_own[pl.ds(i * (tile // LEN) + j, 1), :] = jnp.broadcast_to(gap, (1, 128))
+
+    waits = []
+    for t in range(4):
+        zz = source(t)
+        if t > 0:
+            for m in range(2):
+                z_copy(m, zz, 0).wait_recv()
+        z_forward(zz, lambda copy: copy.start())
+        gather_two(t, zz)
+        gather_three(t, zz, 0, 0)
+        gather_three(t, zz, 0, 1)
+        if t == 0:
+            outs = (policy_out, anchor_out, moment_out, second_out)
+            for a in range(4):
+                copy = pltpu.make_async_copy(
+                    result.at[a, core], outs[a].at[:, mine], local_sem.at[9 + a]
+                )
+                copy.start()
+                waits.append(copy)
+                copy = remote(
+                    result.at[a, 1 - core],
+                    outs[a].at[:, mine],
+                    out_send.at[a],
+                    out_recv.at[a],
+                    mate,
+                )
+                copy.start()
+                waits.append(copy)
+        for m in range(2):
+            gathers[2, t, m].wait_recv()
+            gather_three(t, zz, 1, m)
+        if t > 0:
+            compute(t - 1, source(t - 1))
+    compute(3, source(3))
+
+    copy = remote(score_own, score_pair, m_send.at[0], m_recv.at[0], mate)
+    copy.start()
+    sends.append(copy)
+    copy.wait_recv()
+    table[chip] = (score_own[...] + score_pair[...]) * (1.0 / LEN)
+
+    def table_copy(start, count, slot, device):
+        ref = table.at[pl.ds(start, count)]
+        copy = remote(ref, ref, m_send.at[slot], m_recv.at[slot], device)
+        copy.start()
+        sends.append(copy)
+        return copy
+
+    table_copy(chip, 1, 1, x_mate).wait_recv()
+    table_copy(chip - px, 2, 2, y_mate).wait_recv()
+    last = [table_copy(pz * 4, 4, 2 + s, z_mate(s)) for s in (1, 2, 3)]
+    for copy in last:
+        copy.wait_recv()
+    for copy in waits:
+        copy.wait()
+    for copy in sends:
+        copy.wait_send()
+    for t in range(4):
+        z_forward(source(t), lambda copy: copy.wait_send())
+    margin_out[...] = table[...]
+
+
+def fused_shards(n, tokens, cotangent, policy, anchor, moment, second, readout, pair_index, noisy_flags):
+    tokens_own, depth = tokens.shape
+    rows, channels = policy.shape
+    half = channels // 2
+    block = 2 * rows
+    low = half // 2
+    seq_chip = 2 * tokens_own // LEN
+    sizes = (n, rows, tokens_own, half, depth, seq_chip // 2)
+    bf, f32 = jnp.bfloat16, jnp.float32
+    vmem, dma = pltpu.VMEM, pltpu.SemaphoreType.DMA
+    hbm = pl.BlockSpec(memory_space=pl.ANY)
+    whole = pl.BlockSpec(memory_space=pltpu.VMEM)
+    weight = jax.ShapeDtypeStruct((rows, channels), f32)
+    policy_next, anchor_next, moment_next, second_next, table = pl.pallas_call(
+        functools.partial(fused_kernel, sizes),
+        out_shape=(weight,) * 4 + (jax.ShapeDtypeStruct((n // 2, seq_chip, 128), f32),),
+        in_specs=[hbm] * 6 + [whole],
+        out_specs=(hbm,) * 4 + (whole,),
+        scratch_shapes=[
+            vmem((2, tokens_own, depth), bf),
+            vmem((2, tokens_own, half), bf),
+            vmem((half, 2 * tokens_own), bf),
+            vmem((4, 2, rows, half), f32),
+            vmem((4, 2, low, block), bf),
+            vmem((4, 2, low, block), bf),
+            vmem((4, 2, low, block), f32),
+            vmem((4, 2, low, block), bf),
+            vmem((4, 2, low, block), bf),
+            vmem((4, 2, low, block), f32),
+            vmem((4, low, block), bf),
+            vmem((4, low, block), bf),
+            vmem((4, low, block), bf),
+            vmem((4, low, block), bf),
+            vmem((3, half, block), bf),
+            vmem((3, half, block), bf),
+            vmem((half, block), f32),
+            vmem((4, 2, rows, half), f32),
+            vmem((2, depth, half), bf),
+            vmem((2, 4, tokens_own // 2, half), f32),
+            vmem((seq_chip, 128), f32),
+            vmem((seq_chip, 128), f32),
+            vmem((n // 2, seq_chip, 128), f32),
+            dma((13,)),
+            dma((9,)),
+            dma((9,)),
+            dma((5, 4)),
+            dma((5, 4)),
+            dma((4,)),
+            dma((4,)),
+            dma((2, 2, 4)),
+            dma((2, 4)),
+            dma((4, 2)),
+            dma((4, 2)),
+            dma((4, 2, 2)),
+            dma((4, 2, 2)),
+            dma((6,)),
+            dma((6,)),
+        ],
+        compiler_params=pltpu.CompilerParams(
+            collective_id=0, has_side_effects=True, vmem_limit_bytes=56 * 1024 * 1024
+        ),
+    )(
+        tokens,
+        cotangent,
+        policy,
+        anchor,
+        moment,
+        second,
+        readout.reshape(2, 1, half),
+    )
+    margins = table[:, :, 0].reshape(-1)
+    pair_loss = pair_losses(margins, pair_index, noisy_flags)
     return (policy_next, anchor_next, moment_next, second_next, pair_loss)
 
 
@@ -88,8 +547,12 @@
         P(("rep", "fsdp"), None),
         P(("rep", "fsdp")),
     )
+    n = mesh.shape["fsdp"]
+    body = shards
+    if mesh.shape["rep"] == 1 and n // 8 == len(STEP_ORDER):
+        body = functools.partial(fused_shards, n)
     return jax.shard_map(
-        shards,
+        body,
         mesh=mesh,
         in_specs=placed,
         out_specs=(

time: 349 us -> 97.2 us (0.28)
  waiting for transfers between devices: 266 us -> 0 us
  Pallas kernels: 0 us -> 87.6 us
  blocking collectives: 39.1 us -> 0 us
  matrix products: 25.3 us -> 0 us
  between operations: 13.8 us -> 0.69 us
  local copies, waits for them, and re-layouts: 1.39 us -> 7.89 us
    reduce_scatter x1 -> x0, waiting for transfers between devices: 153 us -> none  [shards(): lax.psum_scatter(lax.dot_general(tokens, cotangent, (((0,), (0,)), ((), (...]
    all_gather x2 -> x0, waiting for transfers between devices: 112 us -> none  [the longest x1 56.8 us: shards(): anchor_whole = lax.all_gather(anchor_half, 'fsdp', axis=0, tiled=True)]
    pallas_call x0 -> x1, Pallas kernels: none -> 87.6 us  [fused_shards(): pl.pallas_call(functools.partial(fused_kernel, sizes), out_shape=(weight,...]
    unnamed x1 -> x0, blocking collectives: 39.1 us -> none
    dot_general x3 -> x0, matrix products: 25.3 us -> none  [the longest x1 8.57 us: shards(): lax.dot_general(tokens, cotangent, (((0,), (0,)), ((), ())), preferred_el...]
    unnamed x19 -> x8, local copies, waits for them, and re-layouts: 1.13 us -> 6.69 us
  transfers between devices with their start and end apart: 3 -> 0, of which waited for: 3 -> 0; matrix products, arithmetic and copies ran while one was open for 2% -> 0% of each run, Pallas kernels for 0% -> 0%
where the time goes in v1:
time: 97.2 us; the launch traced here: 96.9 us
  Pallas kernels  87.6 us (90%)
  local copies, waits for them, and re-layouts  7.89 us (8%)
    pallas_call x1, Pallas kernels, fused_shards(): pl.pallas_call(functools.partial(fused_kernel, sizes), out_shape=(weight,...  87.6 us
    unnamed x8, local copies, waits for them, and re-layouts  6.69 us

profile of v1, /device:TPU:0, one launch (start us, length us, event | category | flops | bytes accessed | tf_op | source)
XLA Modules:
  0.0 96.9 jit_solution(18183008235395337979)
XLA Ops:
  0.6 0.0 copy-start
  0.6 0.0 copy-start.1
  0.7 87.6 %shard_map.128 = (f32[128,512]{1,0:T(8,128)}, f32[128,512]{1,0:T(8,128)}, f32[128,512]{1,0:T(8,128)}, f32[128,512]{1,0:T(8,128)}, f32[16,8,128]{2,1,0:T(8,128)}) custom-call(bf16[768,4096]{1,0:T(8,128)(2,1)} %tokens.1, bf16[768,512]{1,0:T(8,128)(2,1)} %cotangent.1, f32[128,512]{1,0:T(8,128)} %policy.1, f32[128,512]{1,0:T(8,128)} %anchor.1, ...), custom_call_target="tpu_custom_call" | custom-call | tf_op jit(solution)/shard_map/pallas_call | solution.py:476
  88.3 0.9 slice_reduce_fusion
  89.2 0.1 broadcast_in_dim.20
  89.3 0.0 copy-done
  89.3 0.2 slice_reduce_fusion.1
  89.5 0.2 fusion.1
  89.7 0.0 copy-done.1
  89.7 0.5 multiply_subtract_fusion
  90.2 1.7 %copy.18 = f32[128,512]{1,0:T(8,128)} copy(f32[128,512]{1,0:T(8,128)} %get-tuple-element.24) | data formatting | bytes 524288
  91.9 1.7 %copy.19 = f32[128,512]{1,0:T(8,128)} copy(f32[128,512]{1,0:T(8,128)} %get-tuple-element.25) | data formatting | bytes 524288
  93.6 1.7 %copy.20 = f32[128,512]{1,0:T(8,128)} copy(f32[128,512]{1,0:T(8,128)} %get-tuple-element.26) | data formatting | bytes 524288
  95.3 1.7 %copy.21 = f32[128,512]{1,0:T(8,128)} copy(f32[128,512]{1,0:T(8,128)} %get-tuple-element.27) | data formatting | bytes 524288
Async XLA Ops:
  0.6 88.7 %copy-start = (s32[2,2]{1,0:T(2,128)S(1)}, s32[2,2]{1,0:T(2,128)}, u32[]{:S(2)}) copy-start(s32[2,2]{1,0:T(2,128)} %param.16) | copy-start | bytes 52
  0.6 89.0 %copy-start.1 = (s32[2]{0:T(128)S(1)}, s32[2]{0:T(128)}, u32[]{:S(2)}) copy-start(s32[2]{0:T(128)} %param.17) | copy-start | bytes 28

commit v2 on v1

--- a/solution.py
+++ b/solution.py
@@ -1,4 +1,5 @@
 import functools
+import itertools
 import jax
 import jax.numpy as jnp
 from jax import lax
@@ -92,10 +93,7 @@
     moment,
     second,
     readout,
-    policy_out,
-    anchor_out,
-    moment_out,
-    second_out,
+    gradient_out,
     margin_out,
     tok,
     cot,
@@ -117,8 +115,6 @@
     result,
     weights,
     acc,
-    score_own,
-    score_pair,
     table,
     local_sem,
     swap_send,
@@ -129,6 +125,8 @@
     out_recv,
     z_send,
     z_recv,
+    far_send,
+    far_recv,
     g2_send,
     g2_recv,
     g3_send,
@@ -164,7 +162,11 @@
         )
 
     barrier = pltpu.get_barrier_semaphore()
-    others = [mate, x_mate, y_mate] + [z_mate(s) for s in (1, 2, 3)]
+    plane = [
+        me + dc * (1 - 2 * core) + dx * (2 - 4 * px) + dy * (4 - 8 * py)
+        for dc, dx, dy in itertools.product((0, 1), repeat=3)
+    ][1:]
+    others = plane + [z_mate(s) for s in (1, 2, 3)]
     for other in others:
         pl.semaphore_signal(barrier, inc=1, device_id={"fsdp": other}, device_id_type=MESH_ID)
 
@@ -172,18 +174,22 @@
     theirs = pl.ds(pl.multiple_of((1 - core) * half, half), half)
     params = (policy, anchor, moment, second)
 
-    def columns(s):
-        z_to = (pz + s) % 4
-        return pl.ds(pl.multiple_of(z_to * span, span), span)
+    pair = 2 * block
+
+    def columns(s, dy):
+        start = ((pz + s) % 4) * span + ((py + dy) % 2) * pair
+        return pl.ds(pl.multiple_of(start, pair), pair)
+
+    pieces = [(s, dy) for s in STEP_ORDER for dy in (1, 0)]
 
     cot_local = pltpu.make_async_copy(cotangent.at[:, mine], cot.at[core], local_sem.at[4])
     cot_local.start()
     tok_local = {}
-    for s in STEP_ORDER:
-        tok_local[s] = pltpu.make_async_copy(
-            tokens.at[:, columns(s)], tok.at[core, :, columns(s)], local_sem.at[s]
-        )
-        tok_local[s].start()
+    for i, (s, dy) in enumerate(pieces):
+        tok_local[s, dy] = pltpu.make_async_copy(
+            tokens.at[:, columns(s, dy)], tok.at[core, :, columns(s, dy)], local_sem.at[10 + i]
+        )
+        tok_local[s, dy].start()
     par_local = []
     for a in range(4):
         copy = pltpu.make_async_copy(params[a].at[:, mine], par.at[a, core], local_sem.at[5 + a])
@@ -197,16 +203,16 @@
     cot_swap.start()
     sends.append(cot_swap)
     tok_swap = {}
-    for s in STEP_ORDER:
-        tok_swap[s] = remote(
-            tokens.at[:, columns(s)],
-            tok.at[core, :, columns(s)],
-            swap_send.at[s],
-            swap_recv.at[s],
+    for i, (s, dy) in enumerate(pieces):
+        tok_swap[s, dy] = remote(
+            tokens.at[:, columns(s, dy)],
+            tok.at[core, :, columns(s, dy)],
+            swap_send.at[10 + i],
+            swap_recv.at[10 + i],
             mate,
         )
-        tok_swap[s].start()
-        sends.append(tok_swap[s])
+        tok_swap[s, dy].start()
+        sends.append(tok_swap[s, dy])
     par_swap = []
     for a in range(4):
         copy = remote(
@@ -223,9 +229,9 @@
             cot[r].astype(jnp.float32).T.astype(jnp.bfloat16)
         )
 
-    def first(s):
-        tok_local[s].wait()
-        tok_swap[s].wait_recv()
+    def first(s, dy):
+        tok_local[s, dy].wait()
+        tok_swap[s, dy].wait_recv()
 
     def block_gradient(s, dy, dx):
         target = ((pz + s) % 4) * 4 + ((py + dy) % 2) * 2 + (px + dx) % 2
@@ -254,12 +260,13 @@
         sends.append(copy)
 
     def stage_one(s):
-        first(s)
+        first(s, 1)
         block_gradient(s, 1, 1)
+        block_gradient(s, 1, 0)
+        hop("b1", s, 1, send_b1.at[s], recv_b1.at[s], y_mate)
+        first(s, 0)
         block_gradient(s, 0, 1)
         hop("a1", s, 0, send_a1.at[s], recv_a1.at[s], x_mate)
-        block_gradient(s, 1, 0)
-        hop("b1", s, 1, send_b1.at[s], recv_b1.at[s], y_mate)
         block_gradient(s, 0, 0)
 
     def stage_two(s):
@@ -305,8 +312,7 @@
         updated = adam_update(
             gradient[r * rows : (r + 1) * rows], par[0, r], par[1, r], par[2, r], par[3, r]
         )
-        for a in range(4):
-            result[a, r] = updated[a]
+        result[r] = gradient[r * rows : (r + 1) * rows]
         for m in range(2):
             weights[m, pl.ds(pl.multiple_of(home + r * rows, rows), rows), :] = updated[m].astype(
                 jnp.bfloat16
@@ -349,10 +355,28 @@
             gathers[2, t, m] = copy
             sends.append(copy)
 
+    across = 3 - 2 * py - px
+
+    def piece(k, second_half):
+        return pl.ds(pl.multiple_of(k * block + second_half * rows, rows), rows)
+
+    def far_copy(m, zz, s, device):
+        ref = weights.at[m, piece(zz * 4 + across, 1), :]
+        return remote(ref, ref, far_send.at[m, s - 1], far_recv.at[m, zz], device)
+
+    def far_start():
+        for s in (2, 1, 3):
+            for m in range(2):
+                copy = far_copy(m, pz, s, z_mate(s))
+                copy.start()
+                sends.append(copy)
+
     def gather_three(t, zz, late, m):
         ky = (py + late) % 2 if m == 0 else py
         kx = px if m == 0 else (px + late) % 2
         ref = part(m, zz * 4 + ky * 2 + kx)
+        if late == 1 and t > 0:
+            ref = weights.at[m, piece(zz * 4 + ky * 2 + kx, 0), :]
         device = x_mate if m == 0 else y_mate
         copy = remote(ref, ref, g3_send.at[t, late, m], g3_recv.at[t, late, m], device)
         copy.start()
@@ -370,34 +394,61 @@
             product = product * factor[j]
         return jnp.sum(low_part, axis=0) - jnp.log(product)
 
+    def arrived(t, zz, late):
+        for m in range(2):
+            gathers[3, t, late, m].wait_recv()
+            if late == 1 and t > 0:
+                far_copy(m, zz, 1, z_mate(1)).wait_recv()
+
     def compute(t, zz):
-        for late in range(2):
-            for m in range(2):
-                gathers[3, t, late, m].wait_recv()
         where = pl.ds(pl.multiple_of(zz * span, span), span)
 
         @pl.loop(0, 4)
         def _(i):
-            r = i // 2
             at = pl.ds(pl.multiple_of((i % 2) * tile, tile), tile)
-            lhs = tok[r, at, where]
-            values = []
+            lhs = tok[i // 2, at, where]
             for m in range(2):
                 value = jnp.dot(lhs, weights[m, where, :], preferred_element_type=jnp.float32)
-                if t > 0:
-                    value = value + acc[m, i]
-                if t < 3:
-                    acc[m, i] = value
-                else:
-                    acc[m, i] = value * scale
-            if t == 3:
-                for j in range(tile // LEN):
-                    gap = score_sum(acc[0, i, j * LEN : (j + 1) * LEN]) - score_sum(
-                        acc[1, i, j * LEN : (j + 1) * LEN]
+                acc[m, i] = value if t == 0 else acc[m, i] + value
+
+    def spot(zz, dy, dx):
+        k = zz * 4 + ((py + dy) % 2) * 2 + (px + dx) % 2
+        return pl.ds(pl.multiple_of(k * block, block), block)
+
+    def compute_near(zz):
+        @pl.loop(0, 4)
+        def _(i):
+            at = pl.ds(pl.multiple_of((i % 2) * tile, tile), tile)
+            for m in range(2):
+                value = acc[m, i]
+                for dy, dx in ((0, 0), (0, 1), (1, 0)):
+                    where = spot(zz, dy, dx)
+                    value += jnp.dot(
+                        tok[i // 2, at, where],
+                        weights[m, where, :],
+                        preferred_element_type=jnp.float32,
                     )
-                    gap = jnp.sum(gap, axis=0, keepdims=True)
-                    gap = jnp.sum(gap, axis=1, keepdims=True)
-                    score_own[pl.ds(i * (tile // LEN) + j, 1), :] = jnp.broadcast_to(gap, (1, 128))
+                acc[m, i] = value
+
+    def compute_last(zz):
+        where = spot(zz, 1, 1)
+
+        @pl.loop(0, 4)
+        def _(i):
+            at = pl.ds(pl.multiple_of((i % 2) * tile, tile), tile)
+            lhs = tok[i // 2, at, where]
+            for m in range(2):
+                value = jnp.dot(lhs, weights[m, where, :], preferred_element_type=jnp.float32)
+                acc[m, i] = (value + acc[m, i]) * scale
+            for j in range(tile // LEN):
+                gap = score_sum(acc[0, i, j * LEN : (j + 1) * LEN]) - score_sum(
+                    acc[1, i, j * LEN : (j + 1) * LEN]
+                )
+                gap = jnp.sum(gap, axis=0, keepdims=True)
+                gap = jnp.sum(gap, axis=1, keepdims=True)
+                table[core, chip, pl.ds(i * (tile // LEN) + j, 1), :] = jnp.broadcast_to(
+                    gap * (1.0 / LEN), (1, 128)
+                )
 
     waits = []
     for t in range(4):
@@ -410,45 +461,42 @@
         gather_three(t, zz, 0, 0)
         gather_three(t, zz, 0, 1)
         if t == 0:
-            outs = (policy_out, anchor_out, moment_out, second_out)
-            for a in range(4):
-                copy = pltpu.make_async_copy(
-                    result.at[a, core], outs[a].at[:, mine], local_sem.at[9 + a]
-                )
-                copy.start()
-                waits.append(copy)
-                copy = remote(
-                    result.at[a, 1 - core],
-                    outs[a].at[:, mine],
-                    out_send.at[a],
-                    out_recv.at[a],
-                    mate,
-                )
-                copy.start()
-                waits.append(copy)
+            copy = pltpu.make_async_copy(result.at[core], gradient_out.at[:, mine], local_sem.at[9])
+            copy.start()
+            waits.append(copy)
+            copy = remote(
+                result.at[1 - core], gradient_out.at[:, mine], out_send.at[0], out_recv.at[0], mate
+            )
+            copy.start()
+            waits.append(copy)
         for m in range(2):
             gathers[2, t, m].wait_recv()
             gather_three(t, zz, 1, m)
         if t > 0:
+            arrived(t - 1, source(t - 1), 0)
+            arrived(t - 1, source(t - 1), 1)
+            if t == 1:
+                far_start()
             compute(t - 1, source(t - 1))
-    compute(3, source(3))
-
-    copy = remote(score_own, score_pair, m_send.at[0], m_recv.at[0], mate)
-    copy.start()
-    sends.append(copy)
-    copy.wait_recv()
-    table[chip] = (score_own[...] + score_pair[...]) * (1.0 / LEN)
-
-    def table_copy(start, count, slot, device):
-        ref = table.at[pl.ds(start, count)]
+    arrived(3, source(3), 0)
+    compute_near(source(3))
+    arrived(3, source(3), 1)
+    compute_last(source(3))
+
+    def table_copy(ref, slot, device):
         copy = remote(ref, ref, m_send.at[slot], m_recv.at[slot], device)
         copy.start()
         sends.append(copy)
         return copy
 
-    table_copy(chip, 1, 1, x_mate).wait_recv()
-    table_copy(chip - px, 2, 2, y_mate).wait_recv()
-    last = [table_copy(pz * 4, 4, 2 + s, z_mate(s)) for s in (1, 2, 3)]
+    near_copies = [
+        table_copy(table.at[core, pl.ds(chip, 1)], i, device) for i, device in enumerate(plane)
+    ]
+    for copy in near_copies:
+        copy.wait_recv()
+    last = [
+        table_copy(table.at[:, pl.ds(pz * 4, 4)], 6 + s, z_mate(s)) for s in (2, 1, 3)
+    ]
     for copy in last:
         copy.wait_recv()
     for copy in waits:
@@ -458,6 +506,40 @@
     for t in range(4):
         z_forward(source(t), lambda copy: copy.wait_send())
     margin_out[...] = table[...]
+
+
+def finish_kernel(
+    gradient,
+    policy,
+    anchor,
+    moment,
+    second,
+    table,
+    pair_index,
+    noisy_flags,
+    policy_out,
+    anchor_out,
+    moment_out,
+    second_out,
+    loss_out,
+):
+    updated = adam_update(gradient[...], policy[...], anchor[...], moment[...], second[...])
+    for out, value in zip((policy_out, anchor_out, moment_out, second_out), updated):
+        out[...] = value
+    margins = table[0] + table[1]
+    sequence = lax.broadcasted_iota(jnp.int32, margins.shape, 0)
+
+    def margin_of(index):
+        return jnp.sum(jnp.where(sequence == index, margins, 0.0), axis=0, keepdims=True)
+
+    for p in range(noisy_flags.shape[0]):
+        gap = margin_of(pair_index[p, 0]) - margin_of(pair_index[p, 1])
+        gap = jnp.where(noisy_flags[p] == 1, -gap, gap)
+        tail = jnp.log(1.0 + jnp.exp(-jnp.abs(gap)))
+        loss = (1.0 - smoothing) * (tail - jnp.minimum(gap, 0.0)) + smoothing * (
+            tail + jnp.maximum(gap, 0.0)
+        )
+        loss_out[p] = loss[0, 0]
 
 
 def fused_shards(n, tokens, cotangent, policy, anchor, moment, second, readout, pair_index, noisy_flags):
@@ -473,11 +555,11 @@
     hbm = pl.BlockSpec(memory_space=pl.ANY)
     whole = pl.BlockSpec(memory_space=pltpu.VMEM)
     weight = jax.ShapeDtypeStruct((rows, channels), f32)
-    policy_next, anchor_next, moment_next, second_next, table = pl.pallas_call(
+    gradient, table = pl.pallas_call(
         functools.partial(fused_kernel, sizes),
-        out_shape=(weight,) * 4 + (jax.ShapeDtypeStruct((n // 2, seq_chip, 128), f32),),
+        out_shape=(weight, jax.ShapeDtypeStruct((2, n // 2, seq_chip, 128), f32)),
         in_specs=[hbm] * 6 + [whole],
-        out_specs=(hbm,) * 4 + (whole,),
+        out_specs=(hbm, whole),
         scratch_shapes=[
             vmem((2, tokens_own, depth), bf),
             vmem((2, tokens_own, half), bf),
@@ -496,27 +578,27 @@
             vmem((3, half, block), bf),
             vmem((3, half, block), bf),
             vmem((half, block), f32),
-            vmem((4, 2, rows, half), f32),
+            vmem((2, rows, half), f32),
             vmem((2, depth, half), bf),
             vmem((2, 4, tokens_own // 2, half), f32),
-            vmem((seq_chip, 128), f32),
-            vmem((seq_chip, 128), f32),
-            vmem((n // 2, seq_chip, 128), f32),
-            dma((13,)),
-            dma((9,)),
-            dma((9,)),
+            vmem((2, n // 2, seq_chip, 128), f32),
+            dma((18,)),
+            dma((18,)),
+            dma((18,)),
             dma((5, 4)),
             dma((5, 4)),
-            dma((4,)),
-            dma((4,)),
+            dma((1,)),
+            dma((1,)),
             dma((2, 2, 4)),
+            dma((2, 4)),
+            dma((2, 3)),
             dma((2, 4)),
             dma((4, 2)),
             dma((4, 2)),
             dma((4, 2, 2)),
             dma((4, 2, 2)),
-            dma((6,)),
-            dma((6,)),
+            dma((10,)),
+            dma((10,)),
         ],
         compiler_params=pltpu.CompilerParams(
             collective_id=0, has_side_effects=True, vmem_limit_bytes=56 * 1024 * 1024
@@ -530,8 +612,22 @@
         second,
         readout.reshape(2, 1, half),
     )
-    margins = table[:, :, 0].reshape(-1)
-    pair_loss = pair_losses(margins, pair_index, noisy_flags)
+    smem = pl.BlockSpec(memory_space=pltpu.SMEM)
+    policy_next, anchor_next, moment_next, second_next, pair_loss = pl.pallas_call(
+        finish_kernel,
+        out_shape=(weight,) * 4 + (jax.ShapeDtypeStruct(noisy_flags.shape, f32),),
+        in_specs=[whole] * 6 + [smem] * 2,
+        out_specs=(whole,) * 4 + (smem,),
+    )(
+        gradient,
+        policy,
+        anchor,
+        moment,
+        second,
+        table.reshape(2, n // 2 * seq_chip, 128),
+        pair_index,
+        noisy_flags,
+    )
     return (policy_next, anchor_next, moment_next, second_next, pair_loss)
 
 

time: 97.2 us -> 93.7 us (0.964)
  local copies, waits for them, and re-layouts: 7.89 us -> 0 us
  Pallas kernels: 87.6 us -> 92.9 us
    unnamed x8 -> x0, local copies, waits for them, and re-layouts: 6.69 us -> none
    pallas_call x0 -> x1, Pallas kernels: none -> 2.67 us  [fused_shards(): pl.pallas_call(finish_kernel, out_shape=(weight,) * 4 + (jax.ShapeDtypeSt...]
    pallas_call x1, Pallas kernels: 87.6 us -> 90.2 us  [fused_shards(): pl.pallas_call(functools.partial(fused_kernel, sizes), out_shape=(weight,...]
    slice x2 -> x0, local copies, waits for them, and re-layouts: 1.11 us -> none  [the longest x1 0.93 us: fused_shards(): margins = table[:, :, 0].reshape(-1)]
where the time goes in v2:
time: 93.7 us; the launch traced here: 93.5 us
  Pallas kernels  92.9 us (99%)
    pallas_call x1, Pallas kernels, fused_shards(): pl.pallas_call(functools.partial(fused_kernel, sizes), out_shape=(weight,...  90.2 us
    pallas_call x1, Pallas kernels, fused_shards(): pl.pallas_call(finish_kernel, out_shape=(weight,) * 4 + (jax.ShapeDtypeSt...  2.67 us

profile of v2, /device:TPU:0, one launch (start us, length us, event | category | flops | bytes accessed | tf_op | source)
XLA Modules:
  0.0 93.5 jit_solution(2552319503133487883)
XLA Ops:
  0.6 90.2 %shard_map.128 = (f32[128,512]{1,0:T(8,128)}, f32[2,16,8,128]{3,2,1,0:T(8,128)}) custom-call(bf16[768,4096]{1,0:T(8,128)(2,1)} %tokens.1, bf16[768,512]{1,0:T(8,128)(2,1)} %cotangent.1, f32[128,512]{1,0:T(8,128)} %policy.3, f32[128,512]{1,0:T(8,128)} %anchor.3, f32[128,512]{1,0:T(8,128)} %moment.3, f32[128,512]{1,0:T(8,128)} %second.3, f32[2,1,256]{2,1,0:T(1,128)} %bitcast.3), custom_call_target="tpu_custom_call" | custom-call | tf_op jit(solution)/shard_map/pallas_call | solution.py:558
  90.9 2.7 %shard_map.129 = (f32[128,512]{1,0:T(8,128)}, f32[128,512]{1,0:T(8,128)}, f32[128,512]{1,0:T(8,128)}, f32[128,512]{1,0:T(8,128)}, f32[2]{0:T(128)}) custom-call(f32[128,512]{1,0:T(8,128)} %get-tuple-element.7.gradient, f32[128,512]{1,0:T(8,128)} %policy.3, f32[128,512]{1,0:T(8,128)} %anchor.3, f32[128,512]{1,0:T(8,128)} %moment.3, f32[128,512]{1,0:T(8,128)} %second.3, ...), custom_call_target="tpu_custom_call" | custom-call | tf_op jit(solution)/shard_map/pallas_call | solution.py:616

commit v3 on v2

--- a/solution.py
+++ b/solution.py
@@ -125,8 +125,6 @@
     out_recv,
     z_send,
     z_recv,
-    far_send,
-    far_recv,
     g2_send,
     g2_recv,
     g3_send,
@@ -355,35 +353,17 @@
             gathers[2, t, m] = copy
             sends.append(copy)
 
-    across = 3 - 2 * py - px
-
-    def piece(k, second_half):
-        return pl.ds(pl.multiple_of(k * block + second_half * rows, rows), rows)
-
-    def far_copy(m, zz, s, device):
-        ref = weights.at[m, piece(zz * 4 + across, 1), :]
-        return remote(ref, ref, far_send.at[m, s - 1], far_recv.at[m, zz], device)
-
-    def far_start():
-        for s in (2, 1, 3):
-            for m in range(2):
-                copy = far_copy(m, pz, s, z_mate(s))
-                copy.start()
-                sends.append(copy)
-
     def gather_three(t, zz, late, m):
         ky = (py + late) % 2 if m == 0 else py
         kx = px if m == 0 else (px + late) % 2
         ref = part(m, zz * 4 + ky * 2 + kx)
-        if late == 1 and t > 0:
-            ref = weights.at[m, piece(zz * 4 + ky * 2 + kx, 0), :]
         device = x_mate if m == 0 else y_mate
         copy = remote(ref, ref, g3_send.at[t, late, m], g3_recv.at[t, late, m], device)
         copy.start()
         gathers[3, t, late, m] = copy
         sends.append(copy)
 
-    tile = tokens_own // 2
+    tile = tokens_own
     scale = readout[core]
 
     def score_sum(values):
@@ -394,19 +374,17 @@
             product = product * factor[j]
         return jnp.sum(low_part, axis=0) - jnp.log(product)
 
-    def arrived(t, zz, late):
+    def arrived(t, late):
         for m in range(2):
             gathers[3, t, late, m].wait_recv()
-            if late == 1 and t > 0:
-                far_copy(m, zz, 1, z_mate(1)).wait_recv()
 
     def compute(t, zz):
         where = pl.ds(pl.multiple_of(zz * span, span), span)
 
-        @pl.loop(0, 4)
+        @pl.loop(0, 2)
         def _(i):
-            at = pl.ds(pl.multiple_of((i % 2) * tile, tile), tile)
-            lhs = tok[i // 2, at, where]
+            at = pl.ds(0, tile)
+            lhs = tok[i, at, where]
             for m in range(2):
                 value = jnp.dot(lhs, weights[m, where, :], preferred_element_type=jnp.float32)
                 acc[m, i] = value if t == 0 else acc[m, i] + value
@@ -416,15 +394,15 @@
         return pl.ds(pl.multiple_of(k * block, block), block)
 
     def compute_near(zz):
-        @pl.loop(0, 4)
+        @pl.loop(0, 2)
         def _(i):
-            at = pl.ds(pl.multiple_of((i % 2) * tile, tile), tile)
+            at = pl.ds(0, tile)
             for m in range(2):
                 value = acc[m, i]
                 for dy, dx in ((0, 0), (0, 1), (1, 0)):
                     where = spot(zz, dy, dx)
                     value += jnp.dot(
-                        tok[i // 2, at, where],
+                        tok[i, at, where],
                         weights[m, where, :],
                         preferred_element_type=jnp.float32,
                     )
@@ -433,10 +411,10 @@
     def compute_last(zz):
         where = spot(zz, 1, 1)
 
-        @pl.loop(0, 4)
+        @pl.loop(0, 2)
         def _(i):
-            at = pl.ds(pl.multiple_of((i % 2) * tile, tile), tile)
-            lhs = tok[i // 2, at, where]
+            at = pl.ds(0, tile)
+            lhs = tok[i, at, where]
             for m in range(2):
                 value = jnp.dot(lhs, weights[m, where, :], preferred_element_type=jnp.float32)
                 acc[m, i] = (value + acc[m, i]) * scale
@@ -473,14 +451,12 @@
             gathers[2, t, m].wait_recv()
             gather_three(t, zz, 1, m)
         if t > 0:
-            arrived(t - 1, source(t - 1), 0)
-            arrived(t - 1, source(t - 1), 1)
-            if t == 1:
-                far_start()
+            arrived(t - 1, 0)
+            arrived(t - 1, 1)
             compute(t - 1, source(t - 1))
-    arrived(3, source(3), 0)
+    arrived(3, 0)
     compute_near(source(3))
-    arrived(3, source(3), 1)
+    arrived(3, 1)
     compute_last(source(3))
 
     def table_copy(ref, slot, device):
@@ -580,7 +556,7 @@
             vmem((half, block), f32),
             vmem((2, rows, half), f32),
             vmem((2, depth, half), bf),
-            vmem((2, 4, tokens_own // 2, half), f32),
+            vmem((2, 2, tokens_own, half), f32),
             vmem((2, n // 2, seq_chip, 128), f32),
             dma((18,)),
             dma((18,)),
@@ -590,8 +566,6 @@
             dma((1,)),
             dma((1,)),
             dma((2, 2, 4)),
-            dma((2, 4)),
-            dma((2, 3)),
             dma((2, 4)),
             dma((4, 2)),
             dma((4, 2)),

time: 93.7 us -> 87.7 us (0.936)
  Pallas kernels: 92.9 us -> 86.9 us
    pallas_call x1, Pallas kernels: 90.2 us -> 84.2 us  [fused_shards(): pl.pallas_call(functools.partial(fused_kernel, sizes), out_shape=(weight,...]
where the time goes in v3:
time: 87.7 us; the launch traced here: 87.5 us
  Pallas kernels  86.9 us (99%)
    pallas_call x1, Pallas kernels, fused_shards(): pl.pallas_call(functools.partial(fused_kernel, sizes), out_shape=(weight,...  84.2 us
    pallas_call x1, Pallas kernels, fused_shards(): pl.pallas_call(finish_kernel, out_shape=(weight,) * 4 + (jax.ShapeDtypeSt...  2.67 us

profile of v3, /device:TPU:0, one launch (start us, length us, event | category | flops | bytes accessed | tf_op | source)
XLA Modules:
  0.0 87.5 jit_solution(13586398842082387919)
XLA Ops:
  0.6 84.2 %shard_map.128 = (f32[128,512]{1,0:T(8,128)}, f32[2,16,8,128]{3,2,1,0:T(8,128)}) custom-call(bf16[768,4096]{1,0:T(8,128)(2,1)} %tokens.1, bf16[768,512]{1,0:T(8,128)(2,1)} %cotangent.1, f32[128,512]{1,0:T(8,128)} %policy.3, f32[128,512]{1,0:T(8,128)} %anchor.3, f32[128,512]{1,0:T(8,128)} %moment.3, f32[128,512]{1,0:T(8,128)} %second.3, f32[2,1,256]{2,1,0:T(1,128)} %bitcast.3), custom_call_target="tpu_custom_call" | custom-call | tf_op jit(solution)/shard_map/pallas_call | solution.py:534
  84.8 2.7 %shard_map.129 = (f32[128,512]{1,0:T(8,128)}, f32[128,512]{1,0:T(8,128)}, f32[128,512]{1,0:T(8,128)}, f32[128,512]{1,0:T(8,128)}, f32[2]{0:T(128)}) custom-call(f32[128,512]{1,0:T(8,128)} %get-tuple-element.7.gradient, f32[128,512]{1,0:T(8,128)} %policy.3, f32[128,512]{1,0:T(8,128)} %anchor.3, f32[128,512]{1,0:T(8,128)} %moment.3, f32[128,512]{1,0:T(8,128)} %second.3, ...), custom_call_target="tpu_custom_call" | custom-call | tf_op jit(solution)/shard_map/pallas_call | solution.py:590
